TPU v7x, 128 devices: a whole 4x4x4 slice. The times are simulated.
128 devices in a mesh: section: 2 (over x_lo), expert: 16 (over z, x_hi, core), dp: 4 (over y).
Axes of the slice: x: 4 (x_hi: 2, x_lo: 2; x = x_hi * 2 + x_lo), y: 4, z: 4, core: 2. Of those that a mesh axis runs over, the one named last changes fastest.
Arguments:
- fresh_tokens: bfloat16 [2, 4096, 4096], P(None, ('expert', 'dp')), may hold values from -60 to 60
- in_flight: bfloat16 [4096, 4096], P(('expert', 'dp')), may hold values from -60 to 60
- norm_weight: float32 [2, 4096], P('section'), may hold values from 0.1 to 1.9
- gate_up: bfloat16 [2, 16, 2, 4096, 768], P('section', 'expert', None, 'dp'), may hold values from -0.09375 to 0.09375
- down_proj: bfloat16 [2, 16, 768, 4096], P('section', 'expert', 'dp'), may hold values from -0.21875 to 0.21875
- first_moment: bfloat16 [2, 16, 768, 4096], P('section', 'expert', 'dp'), may hold values from -6 to 6
- second_moment: bfloat16 [2, 16, 768, 4096], P('section', 'expert', 'dp'), may hold values from 0.099609375 to 4
- route_ids: int32 [2, 2, 4096, 8], P('section', None, ('expert', 'dp')), may hold values from 0 to 15, all different within a row; in each aligned block of 64 rows (0 to 63, 64 to 127, ..., all dimensions but the last counted through in order) at most 36 rows name the same one
- route_probs: float32 [2, 2, 4096, 8], P('section', None, ('expert', 'dp')), may hold values from 0.05 to 1
- trade_flags: int32 [8, 1], replicated, may hold values from 0 to 1, as said below
Outputs:
- layer_out: bfloat16 [2, 2, 4096, 4096], P('section', None, ('expert', 'dp'))
- gate_up_moved: bfloat16 [2, 16, 2, 4096, 768], P('section', 'expert', None, 'dp')
- down_moved: bfloat16 [2, 16, 768, 4096], P('section', 'expert', 'dp')
- first_moved: bfloat16 [2, 16, 768, 4096], P('section', 'expert', 'dp')
- second_moved: bfloat16 [2, 16, 768, 4096], P('section', 'expert', 'dp')
Inputs may be any that keep to these rules, and one draw needn't show every extreme that they name: `route_ids`: in each aligned block of 64 rows (one device's tokens of one section and tick) the 8 experts of a token differ and no expert is chosen by more than 36 rows. `trade_flags`: at least one entry is 1 and at least one is 0.
All inputs are finite; a program needn't handle non-finite values.
Results may differ from a plain program's by a relative error of at most 0.0035.
Values may be sent and summed in bfloat16 or wider, within the bound.
A program may use at most 128 MiB of HBM per device.

v0:
```python
import jax
import jax.numpy as jnp
from jax import lax
from jax.sharding import PartitionSpec as P

EXPERTS = 16


def partner(value, axis, bit):
    return lax.ppermute(value, axis, [(i, i ^ 1 << bit) for i in range(lax.axis_size(axis))])


def shifted(block, axis, distance):
    devices = range(lax.axis_size(axis))
    route = [(i - distance, i) for i in devices if i - distance in devices]
    return lax.ppermute(block, axis, route)


def rms_normed(inputs, norm_gain):
    values = inputs.astype(jnp.float32)
    inverse_rms = lax.rsqrt(jnp.mean(values * values, axis=-1, keepdims=True) + 1e-06)
    return (values * inverse_rms * norm_gain).astype(jnp.bfloat16)


def per_device(
    fresh_tokens,
    in_flight,
    norm_weight,
    gate_up,
    down_proj,
    first_moment,
    second_moment,
    route_ids,
    route_probs,
    trade_flags,
):
    groups = lax.axis_size("expert")
    half_span = groups // 2
    top_bit = groups.bit_length() - 2
    own_rank = lax.axis_index("expert")
    section_index = lax.axis_index("section")
    full_gate_up = lax.all_gather(gate_up, "dp", axis=3, tiled=True)
    full_down = lax.all_gather(down_proj, "dp", axis=2, tiled=True)
    gate_weights = full_gate_up[0, 0, 0]
    up_weights = full_gate_up[0, 0, 1]
    down_weights = full_down[0, 0]
    expert_ids = jnp.arange(EXPERTS, dtype=jnp.int32)
    probs = route_probs[0]
    mix = probs / jnp.sum(probs, axis=-1, keepdims=True)
    chosen = route_ids[0][:, :, :, None] == expert_ids
    dense_mix = jnp.sum(jnp.where(chosen, mix[:, :, :, None], 0.0), axis=2)
    all_mix = lax.all_gather(dense_mix, "expert", axis=1, tiled=True)
    own_mix = jnp.sum(jnp.where(expert_ids == own_rank, all_mix, 0.0), axis=-1)
    traded = partner((gate_up, down_proj, first_moment, second_moment), "expert", top_bit)

    def layer(inputs, scale, held=None):
        normed = rms_normed(inputs, norm_weight[0])
        arrived = lax.all_gather(normed, "expert", axis=0, tiled=True)
        gate_part = jnp.dot(arrived, gate_weights, preferred_element_type=jnp.float32)
        up_part = jnp.dot(arrived, up_weights, preferred_element_type=jnp.float32)
        active = (jax.nn.silu(gate_part) * up_part).astype(jnp.bfloat16)
        result = jnp.dot(active, down_weights, preferred_element_type=jnp.float32)
        result = (result * scale[:, None]).astype(jnp.bfloat16)
        if held is not None:
            result, held = lax.optimization_barrier((result, held))
        combined = lax.psum_scatter(result, "expert", scatter_dimension=0, tiled=True)
        return (
            (inputs.astype(jnp.float32) + combined.astype(jnp.float32)).astype(jnp.bfloat16),
            held,
        )

    first_input = jnp.where(section_index == 0, fresh_tokens[0], in_flight)
    tick_zero, traded = layer(first_input, own_mix[0], traded)
    arrived = shifted(tick_zero, "section", 1)
    second_input = jnp.where(section_index == 0, fresh_tokens[1], arrived)
    tick_one, _ = layer(second_input, own_mix[1])
    layer_out = jnp.stack([tick_zero, tick_one])[None]
    own_flags = trade_flags[own_rank % half_span] == 1
    mask_five = own_flags[None, :, None, None, None]
    mask_four = own_flags[None, :, None, None]
    gate_up_moved = jnp.where(mask_five, traded[0], gate_up)
    down_moved = jnp.where(mask_four, traded[1], down_proj)
    first_moved = jnp.where(mask_four, traded[2], first_moment)
    second_moved = jnp.where(mask_four, traded[3], second_moment)
    return (layer_out, gate_up_moved, down_moved, first_moved, second_moved)


def solution(mesh):
    return jax.shard_map(
        per_device,
        mesh=mesh,
        in_specs=(
            P(None, ("expert", "dp"), None),
            P(("expert", "dp"), None),
            P("section", None),
            P("section", "expert", None, "dp", None),
            P("section", "expert", "dp", None),
            P("section", "expert", "dp", None),
            P("section", "expert", "dp", None),
            P("section", None, ("expert", "dp"), None),
            P("section", None, ("expert", "dp"), None),
            P(),
        ),
        out_specs=(
            P("section", None, ("expert", "dp"), None),
            P("section", "expert", None, "dp", None),
            P("section", "expert", "dp", None),
            P("section", "expert", "dp", None),
            P("section", "expert", "dp", None),
        ),
        check_vma=False,
    )
```

profile of v0, /device:TPU:0, one launch (start us, length us, event | category | flops | bytes accessed | tf_op | source)
XLA Modules:
  0.0 780.1 jit_solution(14578231850789856475)
XLA Ops:
  7.2 0.0 all-gather.5.cloned.1.call-start
  7.2 1.3 fusion.6
  8.6 0.8 copy-done.2
  9.4 1.8 fusion.8
  11.2 0.0 all-gather.7.cloned.1.call-start
  11.3 0.7 all-gather.7.cloned.1.call-update
  12.0 0.0 all-gather.9.cloned.1.call-start
  12.0 0.7 all-gather.9.cloned.1.call-update
  12.7 0.0 reduce-scatter.3.cloned.1.call-start
  12.8 4.0 collective-permute-start.1
  16.8 0.1 collective-permute-start
  16.9 3.4 collective-permute-start.2
  20.3 0.1 collective-permute-start.3
  20.5 0.1 copy.17
  20.6 35.1 %all_gather.18 = f32[2,1024,16]{2,0,1:T(2,128)S(1)} all-gather(f32[2,64,16]{2,0,1:T(2,128)S(1)} %copy.17), channel_id=1, replica_groups=mesh['section'=2,'expert'=16,'dp'=4] {'expert'}, dimensions={1}, use_global_device_ids=true | all-gather | bytes 139264 | tf_op jit(solution)/shard_map/all_gather | solution.py:52
  55.7 1.2 select_reduce_fusion
  56.9 1.1 fusion.15
  58.0 1.2 copy.20
  59.2 187.8 %all-gather.5.cloned.1.call-done = bf16[1024,4096]{1,0:T(8,128)(2,1)} async-done(((bf16[64,4096]{1,0:T(8,128)(2,1)}), bf16[1024,4096]{1,0:T(8,128)(2,1)}) %all-gather.5.cloned.1.call-update) | async-done | bytes 8388624 | tf_op jit(solution)/shard_map/all_gather | solution.py:58
  247.0 118.0 %all-gather.7.cloned.1.call-done = bf16[1,1,2,4096,768]{4,3,2,1,0:T(8,128)(2,1)} async-done(((bf16[1,1,2,1024,768]{4,3,2,1,0:T(8,128)(2,1)}), bf16[1,1,2,4096,768]{4,3,2,1,0:T(8,128)(2,1)}) %all-gather.7.cloned.1.call-update) | async-done | bytes 12582928 | tf_op jit(solution)/shard_map/all_gather | solution.py:42
  365.0 11.0 %fusion.5 = f32[1024,768]{1,0:T(8,128)S(1)} fusion(bf16[1024,4096]{1,0:T(8,128)(2,1)} %all-gather.5.cloned.1.call-done, bf16[1,1,2,4096,768]{4,3,2,1,0:T(8,128)(2,1)} %all-gather.7.cloned.1.call-done), kind=kOutput, calls=%fused_computation.9 | convolution fusion | flops 6442450944 | bytes 17825792 | tf_op jit(solution)/shard_map/dot_general | solution.py:60
  376.0 0.2 copy-done.13
  376.2 8.1 %multiply_convert_fusion.3 = bf16[1024,768]{1,0:T(8,128)(2,1)} fusion(f32[1024,768]{1,0:T(8,128)S(1)} %fusion.5, bf16[1024,4096]{1,0:T(8,128)(2,1)S(1)} %copy-done.13, bf16[1,1,2,4096,768]{4,3,2,1,0:T(8,128)(2,1)S(1)} %copy-done.12), kind=kOutput, calls=%fused_computation.11 | convolution fusion | flops 6447169536 | bytes 19398656 | tf_op jit(solution)/shard_map/dot_general | solution.py:59
  384.2 49.1 %all-gather.9.cloned.1.call-done = bf16[1,1,768,4096]{3,2,1,0:T(8,128)(2,1)} async-done(((bf16[1,1,192,4096]{3,2,1,0:T(8,128)(2,1)}), bf16[1,1,768,4096]{3,2,1,0:T(8,128)(2,1)}) %all-gather.9.cloned.1.call-update) | async-done | bytes 6291472 | tf_op jit(solution)/shard_map/all_gather | solution.py:43
  433.4 11.2 %multiply_convert_fusion.1 = bf16[1024,4096]{1,0:T(8,128)(2,1)} fusion(f32[1024]{0:T(1024)S(1)} %bitcast.45, bf16[1024,768]{1,0:T(8,128)(2,1)} %multiply_convert_fusion.3, bf16[1,1,768,4096]{3,2,1,0:T(8,128)(2,1)} %all-gather.9.cloned.1.call-done), kind=kOutput, calls=%fused_computation.1 | convolution fusion | flops 6450839552 | bytes 16257024 | tf_op jit(solution)/shard_map/dot_general | solution.py:62
  444.6 0.0 reduce-scatter.3.cloned.1.call-update
  444.7 0.0 all-gather.11.cloned.1.call-start
  444.7 103.2 %reduce-scatter.3.cloned.1.call-done = bf16[64,4096]{1,0:T(8,128)(2,1)} async-done(((bf16[1024,4096]{1,0:T(8,128)(2,1)}), bf16[64,4096]{1,0:T(8,128)(2,1)}) %reduce-scatter.3.cloned.1.call-update) | async-done | bytes 524304 | tf_op jit(solution)/shard_map/reduce_scatter | solution.py:66
  547.9 1.3 fusion.9
  549.3 2.5 collective-permute-start.4
  551.8 10.1 %collective-permute-done.4 = bf16[64,4096]{1,0:T(8,128)(2,1)S(1)} collective-permute-done((bf16[64,4096]{1,0:T(8,128)(2,1)S(1)}, bf16[64,4096]{1,0:T(8,128)(2,1)S(1)}, u32[]{:S(2)}, u32[]{:S(2)}) %collective-permute-start.4) | collective-permute-done | bytes 524320 | tf_op jit(solution)/shard_map/ppermute | solution.py:16
  561.9 1.3 fusion.10
  563.2 0.8 copy-done.3
  564.0 1.0 fusion.12
  565.0 0.2 reduce-scatter.5.cloned.1.call-start
  565.3 1.2 copy.21
  566.5 71.6 %all-gather.11.cloned.1.call-done = bf16[1024,4096]{1,0:T(8,128)(2,1)} async-done(((bf16[64,4096]{1,0:T(8,128)(2,1)}), bf16[1024,4096]{1,0:T(8,128)(2,1)}) %all-gather.11.cloned.1.call-update) | async-done | bytes 8388624 | tf_op jit(solution)/shard_map/all_gather | solution.py:58
  638.1 11.0 %fusion.4 = f32[1024,768]{1,0:T(8,128)S(1)} fusion(bf16[1024,4096]{1,0:T(8,128)(2,1)} %all-gather.11.cloned.1.call-done, bf16[1,1,2,4096,768]{4,3,2,1,0:T(8,128)(2,1)} %all-gather.7.cloned.1.call-done), kind=kOutput, calls=%fused_computation.8 | convolution fusion | flops 6442450944 | bytes 17825792 | tf_op jit(solution)/shard_map/dot_general | solution.py:60
  649.1 9.8 %multiply_convert_fusion.2 = bf16[1024,768]{1,0:T(8,128)(2,1)S(1)} fusion(f32[1024,768]{1,0:T(8,128)S(1)} %fusion.4, bf16[1024,4096]{1,0:T(8,128)(2,1)S(1)} %copy-done.14, bf16[1,1,2,4096,768]{4,3,2,1,0:T(8,128)(2,1)} %all-gather.7.cloned.1.call-done), kind=kOutput, calls=%fused_computation.10 | convolution fusion | flops 6447169536 | bytes 19398656 | tf_op jit(solution)/shard_map/dot_general | solution.py:59
  658.9 11.7 %multiply_convert_fusion = bf16[1024,4096]{1,0:T(8,128)(2,1)} fusion(f32[1024]{0:T(1024)S(1)} %bitcast.46, bf16[1024,768]{1,0:T(8,128)(2,1)S(1)} %multiply_convert_fusion.2, bf16[1,1,768,4096]{3,2,1,0:T(8,128)(2,1)} %all-gather.9.cloned.1.call-done), kind=kOutput, calls=%fused_computation | convolution fusion | flops 6450839552 | bytes 16257024 | tf_op jit(solution)/shard_map/dot_general | solution.py:62
  670.7 0.6 copy-done.15
  671.3 0.6 fusion.16
  671.9 4.6 broadcast_select_fusion
  676.6 4.0 broadcast_select_fusion.3
  680.5 4.9 broadcast_select_fusion.1
  685.4 85.6 %reduce-scatter.5.cloned.1.call-done = bf16[64,4096]{1,0:T(8,128)(2,1)} async-done(((bf16[1024,4096]{1,0:T(8,128)(2,1)}), bf16[64,4096]{1,0:T(8,128)(2,1)}) %reduce-scatter.5.cloned.1.call-update) | async-done | bytes 524304 | tf_op jit(solution)/shard_map/reduce_scatter | solution.py:66
  771.0 1.2 fusion.14
  772.2 1.1 maximum_bitcast_fusion
  (41 shorter events, 0.2 us)
Async XLA Ops:
  7.2 239.8 %all-gather.5.cloned.1.call-start = ((), (), s32[]{:S(2)}) async-start(), calls=%async_computation.2 | async-start | bytes 8912896 | tf_op jit(solution)/shard_map/all_gather | solution.py:58
  8.6 0.8 copy-start.2
  9.4 7.5 copy-start
  9.4 11.1 %copy-start.10 = (f32[1,2,64,8]{2,3,1,0:T(8,128)S(1)}, f32[1,2,64,8]{2,3,1,0:T(8,128)}, u32[]{:S(2)}) copy-start(f32[1,2,64,8]{2,3,1,0:T(8,128)} %param.18) | copy-start | bytes 12292
  9.4 11.1 %copy-start.11 = (s32[1,2,64,8]{2,3,1,0:T(8,128)S(1)}, s32[1,2,64,8]{2,3,1,0:T(8,128)}, u32[]{:S(2)}) copy-start(s32[1,2,64,8]{2,3,1,0:T(8,128)} %param.17) | copy-start | bytes 12292
  11.2 353.7 %all-gather.7.cloned.1.call-start = ((), (), s32[]{:S(2)}) async-start(), calls=%async_computation.3 | async-start | bytes 15728640 | tf_op jit(solution)/shard_map/all_gather | solution.py:42
  12.0 421.4 %all-gather.9.cloned.1.call-start = ((), (), s32[]{:S(2)}) async-start(), calls=%async_computation.4 | async-start | bytes 7864320 | tf_op jit(solution)/shard_map/all_gather | solution.py:43
  12.7 535.2 %reduce-scatter.3.cloned.1.call-start = ((), (), s32[]{:S(2)}) async-start(), calls=%async_computation.5 | async-start | bytes 8912896 | tf_op jit(solution)/shard_map/reduce_scatter | solution.py:66
  12.8 431.9 %collective-permute-start.1 = (bf16[1,1,192,4096]{3,2,1,0:T(8,128)(2,1)}, bf16[1,1,192,4096]{3,2,1,0:T(8,128)(2,1)}, u32[]{:S(2)}, u32[]{:S(2)}) collective-permute-start(bf16[1,1,192,4096]{3,2,1,0:T(8,128)(2,1)} %param.14), channel_id=1, source_target_pairs={{0,32},{4,36},{8,40},{12,44},{16,48},{20,52},{24,56},{28,60},{32,0... | collective-permute-start | bytes 4718600 | tf_op jit(solution)/shard_map/ppermute | solution.py:10
  16.8 427.8 %collective-permute-start = (bf16[1,1,2,1024,768]{4,3,2,1,0:T(8,128)(2,1)S(1)}, bf16[1,1,2,1024,768]{4,3,2,1,0:T(8,128)(2,1)}, u32[]{:S(2)}, u32[]{:S(2)}) collective-permute-start(bf16[1,1,2,1024,768]{4,3,2,1,0:T(8,128)(2,1)S(1)} %copy-done), channel_id=1, source_target_pairs={{0,32},{4,36},{8,40},{12,44},{16,48},{20,52},{24,56},{28,60},{32,0... | collective-permute-start | bytes 9437192 | tf_op jit(solution)/shard_map/ppermute | solution.py:10
  16.9 427.7 %collective-permute-start.2 = (bf16[1,1,192,4096]{3,2,1,0:T(8,128)(2,1)}, bf16[1,1,192,4096]{3,2,1,0:T(8,128)(2,1)}, u32[]{:S(2)}, u32[]{:S(2)}) collective-permute-start(bf16[1,1,192,4096]{3,2,1,0:T(8,128)(2,1)} %param.15), channel_id=1, source_target_pairs={{0,32},{4,36},{8,40},{12,44},{16,48},{20,52},{24,56},{28,60},{32,0... | collective-permute-start | bytes 4718600 | tf_op jit(solution)/shard_map/ppermute | solution.py:10
  20.3 424.3 %collective-permute-start.3 = (bf16[1,1,192,4096]{3,2,1,0:T(8,128)(2,1)}, bf16[1,1,192,4096]{3,2,1,0:T(8,128)(2,1)}, u32[]{:S(2)}, u32[]{:S(2)}) collective-permute-start(bf16[1,1,192,4096]{3,2,1,0:T(8,128)(2,1)} %param.16), channel_id=1, source_target_pairs={{0,32},{4,36},{8,40},{12,44},{16,48},{20,52},{24,56},{28,60},{32,0... | collective-permute-start | bytes 4718600 | tf_op jit(solution)/shard_map/ppermute | solution.py:10
  365.0 11.0 %copy-start.12 = (bf16[1,1,2,4096,768]{4,3,2,1,0:T(8,128)(2,1)S(1)}, bf16[1,1,2,4096,768]{4,3,2,1,0:T(8,128)(2,1)}, u32[]{:S(2)}) copy-start(bf16[1,1,2,4096,768]{4,3,2,1,0:T(8,128)(2,1)} %all-gather.7.cloned.1.call-done) | copy-start | bytes 37748740
  365.0 11.2 %copy-start.13 = (bf16[1024,4096]{1,0:T(8,128)(2,1)S(1)}, bf16[1024,4096]{1,0:T(8,128)(2,1)}, u32[]{:S(2)}) copy-start(bf16[1024,4096]{1,0:T(8,128)(2,1)} %all-gather.5.cloned.1.call-done) | copy-start | bytes 25165828
  444.7 119.3 %copy-start.9 = (f32[1,4096]{1,0:T(1,128)S(1)}, f32[1,4096]{1,0:T(1,128)}, u32[]{:S(2)}) copy-start(f32[1,4096]{1,0:T(1,128)} %param.12) | copy-start | bytes 49156
  444.7 193.4 %all-gather.11.cloned.1.call-start = ((), (), s32[]{:S(2)}) async-start(), calls=%async_computation.6 | async-start | bytes 8912896 | tf_op jit(solution)/shard_map/all_gather | solution.py:58
  549.3 2.5 copy-start.5
  549.3 12.6 %collective-permute-start.4 = (bf16[64,4096]{1,0:T(8,128)(2,1)S(1)}, bf16[64,4096]{1,0:T(8,128)(2,1)S(1)}, u32[]{:S(2)}, u32[]{:S(2)}) collective-permute-start(bf16[64,4096]{1,0:T(8,128)(2,1)S(1)} %fusion.9), channel_id=1, source_target_pairs={{0,64},{1,65},{2,66},{3,67},{4,68},{5,69},{6,70},{7,71},{8,72},{9,... | collective-permute-start | bytes 1572872 | tf_op jit(solution)/shard_map/ppermute | solution.py:16
  563.2 0.8 copy-start.3
  565.0 206.0 %reduce-scatter.5.cloned.1.call-start = ((), (), s32[]{:S(2)}) async-start(), calls=%async_computation.7 | async-start | bytes 8912896 | tf_op jit(solution)/shard_map/reduce_scatter | solution.py:66
  638.1 11.1 %copy-start.14 = (bf16[1024,4096]{1,0:T(8,128)(2,1)S(1)}, bf16[1024,4096]{1,0:T(8,128)(2,1)}, u32[]{:S(2)}) copy-start(bf16[1024,4096]{1,0:T(8,128)(2,1)} %all-gather.11.cloned.1.call-done) | copy-start | bytes 25165828
  670.7 0.7 copy-start.15
  671.9 4.7 copy-start.1
  676.6 4.0 copy-start.7
  676.6 4.0 copy-start.8
  680.5 90.5 %copy-start.4 = (bf16[64,4096]{1,0:T(8,128)(2,1)S(1)}, bf16[64,4096]{1,0:T(8,128)(2,1)}, u32[]{:S(2)}) copy-start(bf16[64,4096]{1,0:T(8,128)(2,1)} %copy-done.3) | copy-start | bytes 1572868
  680.5 91.6 %copy-start.6 = (bf16[64,4096]{1,0:T(8,128)(2,1)S(1)}, bf16[64,4096]{1,0:T(8,128)(2,1)}, u32[]{:S(2)}) copy-start(bf16[64,4096]{1,0:T(8,128)(2,1)} %copy-done.5) | copy-start | bytes 1572868
Sparse Core Ops, SparseCore 0:
  11.4 235.5 all-gather.4
  248.6 116.2 all-gather.6
  366.6 66.6 all-gather.8
  444.8 103.1 reduce-scatter.2
  565.1 72.8 all-gather.10
  670.8 100.1 reduce-scatter.4
where the time goes:
time: 781 us; the launch traced here: 780 us
  waiting for transfers between devices  627 us (80%)
  matrix products  62.9 us (8%)
  blocking collectives  35.1 us (4%)
  other arithmetic  24.4 us (3%)
  between operations  14.3 us (2%)
  starting transfers between devices  10.6 us (1%)
    all_gather x2, waiting for transfers between devices, layer(): arrived = lax.all_gather(normed, 'expert', axis=0, tiled=True)  259 us
    reduce_scatter x2, waiting for transfers between devices, layer(): lax.psum_scatter(result, 'expert', scatter_dimension=0, tiled=True)  189 us
    all_gather x1, waiting for transfers between devices, per_device(): full_gate_up = lax.all_gather(gate_up, 'dp', axis=3, tiled=True)  118 us
    all_gather x1, waiting for transfers between devices, per_device(): full_down = lax.all_gather(down_proj, 'dp', axis=2, tiled=True)  49.1 us
    all_gather x1, blocking collectives, per_device(): all_mix = lax.all_gather(dense_mix, 'expert', axis=1, tiled=True)  35.1 us
    dot_general x2, matrix products, layer(): result = jnp.dot(active, down_weights, preferred_element_type=jnp.float32)  23 us
    dot_general x2, matrix products, layer(): up_part = jnp.dot(arrived, up_weights, preferred_element_type=jnp.float32)  22.1 us
    dot_general x2, matrix products, layer(): jnp.dot(arrived, gate_weights, preferred_element_type=jnp.float32)  17.8 us
  transfers between devices with their start and end apart: 11, of which 7 were waited for; matrix products, arithmetic and copies ran while one was open for 6% of the time, Pallas kernels for 0%

commit v1 on v0

--- a/solution.py
+++ b/solution.py
@@ -55,7 +55,9 @@
 
     def layer(inputs, scale, held=None):
         normed = rms_normed(inputs, norm_weight[0])
-        arrived = lax.all_gather(normed, "expert", axis=0, tiled=True)
+        arrived = jnp.concatenate(
+            lax.all_to_all(jnp.stack([normed] * lax.axis_size("expert")), "expert", 0, 0), axis=0
+        )
         gate_part = jnp.dot(arrived, gate_weights, preferred_element_type=jnp.float32)
         up_part = jnp.dot(arrived, up_weights, preferred_element_type=jnp.float32)
         active = (jax.nn.silu(gate_part) * up_part).astype(jnp.bfloat16)

time: 781 us -> 687 us (0.88)
  waiting for transfers between devices: 627 us -> 437 us
  blocking collectives: 35.1 us -> 109 us
  starting transfers between devices: 10.6 us -> 23.1 us
  local copies, waits for them, and re-layouts: 6.06 us -> 14.9 us
    all_gather x2 -> x0, waiting for transfers between devices: 259 us -> none  [layer(): arrived = lax.all_gather(normed, 'expert', axis=0, tiled=True)]
    all_gather x1, waiting for transfers between devices: 118 us -> 0.01 us  [per_device(): full_gate_up = lax.all_gather(gate_up, 'dp', axis=3, tiled=True)]
    all_to_all x0 -> x2, waiting for transfers between devices: none -> 95.3 us  [layer(): lax.all_to_all(jnp.stack([normed] * lax.axis_size('expert')), 'expert', 0...]
    ppermute x4, waiting for transfers between devices: 0.01 us -> 81.4 us  [partner(): lax.ppermute(value, axis, [(i, i ^ 1 << bit) for i in range(lax.axis_size...]
    all_gather x1, blocking collectives: 35.1 us -> 109 us  [per_device(): all_mix = lax.all_gather(dense_mix, 'expert', axis=1, tiled=True)]
    reduce_scatter x2, waiting for transfers between devices: 189 us -> 215 us  [layer(): lax.psum_scatter(result, 'expert', scatter_dimension=0, tiled=True)]
    all_gather x1, waiting for transfers between devices: 49.1 us -> 34.2 us  [per_device(): full_down = lax.all_gather(down_proj, 'dp', axis=2, tiled=True)]
    all_to_all x0 -> x2, starting transfers between devices: none -> 13.1 us  [layer(): lax.all_to_all(jnp.stack([normed] * lax.axis_size('expert')), 'expert', 0...]
  transfers between devices with their start and end apart: 11 -> 11, of which waited for: 7 -> 7; matrix products, arithmetic and copies ran while one was open for 6% -> 8% of each run, Pallas kernels for 0% -> 0%
where the time goes in v1:
time: 687 us; the launch traced here: 686 us
  waiting for transfers between devices  437 us (64%)
  blocking collectives  109 us (16%)
  matrix products  67.5 us (10%)
  starting transfers between devices  23.1 us (3%)
  other arithmetic  21 us (3%)
  local copies, waits for them, and re-layouts  14.9 us (2%)
  between operations  14 us (2%)
    reduce_scatter x2, waiting for transfers between devices, layer(): lax.psum_scatter(result, 'expert', scatter_dimension=0, tiled=True)  215 us
    all_gather x1, blocking collectives, per_device(): all_mix = lax.all_gather(dense_mix, 'expert', axis=1, tiled=True)  109 us
    all_to_all x2, waiting for transfers between devices, layer(): lax.all_to_all(jnp.stack([normed] * lax.axis_size('expert')), 'expert', 0...  95.3 us
    ppermute x4, waiting for transfers between devices, partner(): lax.ppermute(value, axis, [(i, i ^ 1 << bit) for i in range(lax.axis_size...  81.4 us
    all_gather x1, waiting for transfers between devices, per_device(): full_down = lax.all_gather(down_proj, 'dp', axis=2, tiled=True)  34.2 us
    dot_general x2, matrix products, layer(): result = jnp.dot(active, down_weights, preferred_element_type=jnp.float32)  23 us
    dot_general x2, matrix products, layer(): up_part = jnp.dot(arrived, up_weights, preferred_element_type=jnp.float32)  23 us
    dot_general x2, matrix products, layer(): jnp.dot(arrived, gate_weights, preferred_element_type=jnp.float32)  21.6 us
  transfers between devices with their start and end apart: 11, of which 7 were waited for; matrix products, arithmetic and copies ran while one was open for 8% of the time, Pallas kernels for 0%

profile of v1, /device:TPU:0, one launch (start us, length us, event | category | flops | bytes accessed | tf_op | source)
XLA Modules:
  0.0 686.0 jit_solution(11759080795299822149)
XLA Ops:
  7.2 0.7 all-gather.3.cloned.1.call-update
  7.9 0.5 copy-done.9
  8.4 0.1 copy-done.10
  8.5 0.3 fusion.6
  8.8 0.2 fusion.8
  9.0 0.6 copy-done.2
  9.6 4.3 stack.10
  13.9 8.3 %all-to-all-start = ((bf16[16,64,4096]{2,1,0:T(8,128)(2,1)}), bf16[16,64,4096]{2,1,0:T(8,128)(2,1)}, u32[]{:S(2)}, u32[]{:S(2)}) async-start(bf16[16,64,4096]{2,1,0:T(8,128)(2,1)} %stack.10), calls=%async_computation | async-start | bytes 16777216 | tf_op jit(solution)/shard_map/all_to_all | solution.py:59
  22.2 0.0 all-gather.5.cloned.1.call-start
  22.3 0.7 all-gather.5.cloned.1.call-update
  23.0 3.5 collective-permute-start.1
  26.5 0.2 collective-permute-start
  26.6 3.4 collective-permute-start.2
  30.0 0.2 collective-permute-start.3
  30.2 0.1 copy.17
  30.3 108.6 %all_gather.11 = f32[2,1024,16]{2,0,1:T(2,128)S(1)} all-gather(f32[2,64,16]{2,0,1:T(2,128)S(1)} %copy.17), channel_id=1, replica_groups=mesh['section'=2,'expert'=16,'dp'=4] {'expert'}, dimensions={1}, use_global_device_ids=true | all-gather | bytes 139264 | tf_op jit(solution)/shard_map/all_gather | solution.py:52
  139.0 1.2 select_reduce_fusion
  140.1 1.1 fusion.15
  141.2 1.3 copy.20
  142.5 12.1 %fusion.5 = f32[1024,768]{1,0:T(8,128)S(1)} fusion(bf16[1024,4096]{1,0:T(8,128)(2,1)} %bitcast.2, bf16[1,1,2,4096,768]{4,3,2,1,0:T(8,128)(2,1)} %all-gather.3.cloned.1.call-done), kind=kOutput, calls=%fused_computation.9 | convolution fusion | flops 6442450944 | bytes 17825792 | tf_op jit(solution)/shard_map/dot_general | solution.py:62
  154.6 10.4 %multiply_convert_fusion.3 = bf16[1024,768]{1,0:T(8,128)(2,1)} fusion(f32[1024,768]{1,0:T(8,128)S(1)} %fusion.5, bf16[1024,4096]{1,0:T(8,128)(2,1)} %bitcast.2, bf16[1,1,2,4096,768]{4,3,2,1,0:T(8,128)(2,1)S(1)} %copy-done.14), kind=kOutput, calls=%fused_computation.11 | convolution fusion | flops 6447169536 | bytes 19398656 | tf_op jit(solution)/shard_map/dot_general | solution.py:61
  165.0 34.2 %all-gather.5.cloned.1.call-done = bf16[1,1,768,4096]{3,2,1,0:T(8,128)(2,1)} async-done(((bf16[1,1,192,4096]{3,2,1,0:T(8,128)(2,1)}), bf16[1,1,768,4096]{3,2,1,0:T(8,128)(2,1)}) %all-gather.5.cloned.1.call-update) | async-done | bytes 6291472 | tf_op jit(solution)/shard_map/all_gather | solution.py:43
  199.2 11.3 %multiply_convert_fusion.1 = bf16[1024,4096]{1,0:T(8,128)(2,1)} fusion(f32[1024]{0:T(1024)S(1)} %bitcast.47, bf16[1024,768]{1,0:T(8,128)(2,1)} %multiply_convert_fusion.3, bf16[1,1,768,4096]{3,2,1,0:T(8,128)(2,1)} %all-gather.5.cloned.1.call-done), kind=kOutput, calls=%fused_computation.1 | convolution fusion | flops 6450839552 | bytes 16257024 | tf_op jit(solution)/shard_map/dot_general | solution.py:64
  210.4 48.1 %collective-permute-done.2 = bf16[1,1,192,4096]{3,2,1,0:T(8,128)(2,1)} collective-permute-done((bf16[1,1,192,4096]{3,2,1,0:T(8,128)(2,1)}, bf16[1,1,192,4096]{3,2,1,0:T(8,128)(2,1)}, u32[]{:S(2)}, u32[]{:S(2)}) %collective-permute-start.2) | collective-permute-done | bytes 1572896 | tf_op jit(solution)/shard_map/ppermute | solution.py:10
  258.6 33.2 %collective-permute-done.3 = bf16[1,1,192,4096]{3,2,1,0:T(8,128)(2,1)} collective-permute-done((bf16[1,1,192,4096]{3,2,1,0:T(8,128)(2,1)}, bf16[1,1,192,4096]{3,2,1,0:T(8,128)(2,1)}, u32[]{:S(2)}, u32[]{:S(2)}) %collective-permute-start.3) | collective-permute-done | bytes 1572896 | tf_op jit(solution)/shard_map/ppermute | solution.py:10
  291.8 127.6 %reduce-scatter.3.cloned.1.call-done = bf16[64,4096]{1,0:T(8,128)(2,1)} async-done(((bf16[1024,4096]{1,0:T(8,128)(2,1)}), bf16[64,4096]{1,0:T(8,128)(2,1)}) %reduce-scatter.3.cloned.1.call-update) | async-done | bytes 524304 | tf_op jit(solution)/shard_map/reduce_scatter | solution.py:68
  419.4 1.3 fusion.9
  420.8 2.5 collective-permute-start.4
  423.3 10.1 %collective-permute-done.4 = bf16[64,4096]{1,0:T(8,128)(2,1)S(1)} collective-permute-done((bf16[64,4096]{1,0:T(8,128)(2,1)S(1)}, bf16[64,4096]{1,0:T(8,128)(2,1)S(1)}, u32[]{:S(2)}, u32[]{:S(2)}) %collective-permute-start.4) | collective-permute-done | bytes 524320 | tf_op jit(solution)/shard_map/ppermute | solution.py:16
  433.4 1.3 fusion.10
  434.7 0.8 copy-done.3
  435.5 0.2 fusion.12
  435.7 4.3 stack.12
  440.0 4.8 all-to-all-start.1
  444.8 0.3 reduce-scatter.5.cloned.1.call-start
  445.1 1.2 copy.21
  446.3 95.3 %all-to-all-done.1 = bf16[16,64,4096]{2,1,0:T(8,128)(2,1)} async-done(((bf16[16,64,4096]{2,1,0:T(8,128)(2,1)}), bf16[16,64,4096]{2,1,0:T(8,128)(2,1)}, u32[]{:S(2)}, u32[]{:S(2)}) %all-to-all-start.1) | async-done | bytes 8388640 | tf_op jit(solution)/shard_map/all_to_all | solution.py:59
  541.5 10.9 %fusion.4 = f32[1024,768]{1,0:T(8,128)S(1)} fusion(bf16[1024,4096]{1,0:T(8,128)(2,1)} %bitcast.11, bf16[1,1,2,4096,768]{4,3,2,1,0:T(8,128)(2,1)} %all-gather.3.cloned.1.call-done), kind=kOutput, calls=%fused_computation.8 | convolution fusion | flops 6442450944 | bytes 17825792 | tf_op jit(solution)/shard_map/dot_general | solution.py:62
  552.5 11.2 %multiply_convert_fusion.2 = bf16[1024,768]{1,0:T(8,128)(2,1)S(1)} fusion(f32[1024,768]{1,0:T(8,128)S(1)} %fusion.4, bf16[1024,4096]{1,0:T(8,128)(2,1)} %bitcast.11, bf16[1,1,2,4096,768]{4,3,2,1,0:T(8,128)(2,1)} %all-gather.3.cloned.1.call-done), kind=kOutput, calls=%fused_computation.10 | convolution fusion | flops 6447169536 | bytes 19398656 | tf_op jit(solution)/shard_map/dot_general | solution.py:61
  563.7 11.7 %multiply_convert_fusion = bf16[1024,4096]{1,0:T(8,128)(2,1)} fusion(f32[1024]{0:T(1024)S(1)} %bitcast.48, bf16[1024,768]{1,0:T(8,128)(2,1)S(1)} %multiply_convert_fusion.2, bf16[1,1,768,4096]{3,2,1,0:T(8,128)(2,1)} %all-gather.5.cloned.1.call-done), kind=kOutput, calls=%fused_computation | convolution fusion | flops 6450839552 | bytes 16257024 | tf_op jit(solution)/shard_map/dot_general | solution.py:64
  575.5 0.6 copy-done.15
  576.1 0.6 fusion.16
  576.7 4.6 broadcast_select_fusion
  581.3 4.0 broadcast_select_fusion.3
  585.4 4.9 broadcast_select_fusion.1
  590.3 86.9 %reduce-scatter.5.cloned.1.call-done = bf16[64,4096]{1,0:T(8,128)(2,1)} async-done(((bf16[1024,4096]{1,0:T(8,128)(2,1)}), bf16[64,4096]{1,0:T(8,128)(2,1)}) %reduce-scatter.5.cloned.1.call-update) | async-done | bytes 524304 | tf_op jit(solution)/shard_map/reduce_scatter | solution.py:68
  677.2 1.2 fusion.14
  678.4 1.1 maximum_bitcast_fusion
  (41 shorter events, 0.3 us)
Async XLA Ops:
  7.2 1.2 copy-start.9
  7.2 1.3 copy-start.10
  7.2 1.7 copy-start.11
  7.2 135.3 %all-gather.3.cloned.1.call-start = ((), (), s32[]{:S(2)}) async-start(), calls=%async_computation.4 | async-start | bytes 15728640 | tf_op jit(solution)/shard_map/all_gather | solution.py:42
  8.8 0.8 copy-start.2
  13.9 12.5 %copy-start = (bf16[1,1,2,1024,768]{4,3,2,1,0:T(8,128)(2,1)S(1)}, bf16[1,1,2,1024,768]{4,3,2,1,0:T(8,128)(2,1)}, u32[]{:S(2)}) copy-start(bf16[1,1,2,1024,768]{4,3,2,1,0:T(8,128)(2,1)} %param.13) | copy-start | bytes 9437188
  13.9 16.2 %copy-start.12 = (f32[1,2,64,8]{2,3,1,0:T(8,128)S(1)}, f32[1,2,64,8]{2,3,1,0:T(8,128)}, u32[]{:S(2)}) copy-start(f32[1,2,64,8]{2,3,1,0:T(8,128)} %param.18) | copy-start | bytes 12292
  13.9 16.3 %copy-start.13 = (s32[1,2,64,8]{2,3,1,0:T(8,128)S(1)}, s32[1,2,64,8]{2,3,1,0:T(8,128)}, u32[]{:S(2)}) copy-start(s32[1,2,64,8]{2,3,1,0:T(8,128)} %param.17) | copy-start | bytes 12292
  13.9 128.6 %all-to-all-start = ((bf16[16,64,4096]{2,1,0:T(8,128)(2,1)}), bf16[16,64,4096]{2,1,0:T(8,128)(2,1)}, u32[]{:S(2)}, u32[]{:S(2)}) async-start(bf16[16,64,4096]{2,1,0:T(8,128)(2,1)} %stack.10), calls=%async_computation | async-start | bytes 16777216 | tf_op jit(solution)/shard_map/all_to_all | solution.py:59
  22.2 177.0 %all-gather.5.cloned.1.call-start = ((), (), s32[]{:S(2)}) async-start(), calls=%async_computation.5 | async-start | bytes 7864320 | tf_op jit(solution)/shard_map/all_gather | solution.py:43
  23.0 396.4 %reduce-scatter.3.cloned.1.call-start = ((), (), s32[]{:S(2)}) async-start(), calls=%async_computation.6 | async-start | bytes 8912896 | tf_op jit(solution)/shard_map/reduce_scatter | solution.py:68
  23.0 268.8 %collective-permute-start.1 = (bf16[1,1,192,4096]{3,2,1,0:T(8,128)(2,1)}, bf16[1,1,192,4096]{3,2,1,0:T(8,128)(2,1)}, u32[]{:S(2)}, u32[]{:S(2)}) collective-permute-start(bf16[1,1,192,4096]{3,2,1,0:T(8,128)(2,1)} %param.14), channel_id=1, source_target_pairs={{0,32},{4,36},{8,40},{12,44},{16,48},{20,52},{24,56},{28,60},{32,0... | collective-permute-start | bytes 4718600 | tf_op jit(solution)/shard_map/ppermute | solution.py:10
  26.5 265.3 %collective-permute-start = (bf16[1,1,2,1024,768]{4,3,2,1,0:T(8,128)(2,1)S(1)}, bf16[1,1,2,1024,768]{4,3,2,1,0:T(8,128)(2,1)}, u32[]{:S(2)}, u32[]{:S(2)}) collective-permute-start(bf16[1,1,2,1024,768]{4,3,2,1,0:T(8,128)(2,1)S(1)} %copy-done), channel_id=1, source_target_pairs={{0,32},{4,36},{8,40},{12,44},{16,48},{20,52},{24,56},{28,60},{32,0... | collective-permute-start | bytes 9437192 | tf_op jit(solution)/shard_map/ppermute | solution.py:10
  26.6 231.9 %collective-permute-start.2 = (bf16[1,1,192,4096]{3,2,1,0:T(8,128)(2,1)}, bf16[1,1,192,4096]{3,2,1,0:T(8,128)(2,1)}, u32[]{:S(2)}, u32[]{:S(2)}) collective-permute-start(bf16[1,1,192,4096]{3,2,1,0:T(8,128)(2,1)} %param.15), channel_id=1, source_target_pairs={{0,32},{4,36},{8,40},{12,44},{16,48},{20,52},{24,56},{28,60},{32,0... | collective-permute-start | bytes 4718600 | tf_op jit(solution)/shard_map/ppermute | solution.py:10
  30.0 261.8 %collective-permute-start.3 = (bf16[1,1,192,4096]{3,2,1,0:T(8,128)(2,1)}, bf16[1,1,192,4096]{3,2,1,0:T(8,128)(2,1)}, u32[]{:S(2)}, u32[]{:S(2)}) collective-permute-start(bf16[1,1,192,4096]{3,2,1,0:T(8,128)(2,1)} %param.16), channel_id=1, source_target_pairs={{0,32},{4,36},{8,40},{12,44},{16,48},{20,52},{24,56},{28,60},{32,0... | collective-permute-start | bytes 4718600 | tf_op jit(solution)/shard_map/ppermute | solution.py:10
  142.5 12.1 %copy-start.14 = (bf16[1,1,2,4096,768]{4,3,2,1,0:T(8,128)(2,1)S(1)}, bf16[1,1,2,4096,768]{4,3,2,1,0:T(8,128)(2,1)}, u32[]{:S(2)}) copy-start(bf16[1,1,2,4096,768]{4,3,2,1,0:T(8,128)(2,1)} %all-gather.3.cloned.1.call-done) | copy-start | bytes 37748740
  420.8 2.5 copy-start.5
  420.8 12.6 %collective-permute-start.4 = (bf16[64,4096]{1,0:T(8,128)(2,1)S(1)}, bf16[64,4096]{1,0:T(8,128)(2,1)S(1)}, u32[]{:S(2)}, u32[]{:S(2)}) collective-permute-start(bf16[64,4096]{1,0:T(8,128)(2,1)S(1)} %fusion.9), channel_id=1, source_target_pairs={{0,64},{1,65},{2,66},{3,67},{4,68},{5,69},{6,70},{7,71},{8,72},{9,... | collective-permute-start | bytes 1572872 | tf_op jit(solution)/shard_map/ppermute | solution.py:16
  434.7 0.8 copy-start.3
  440.0 101.6 %all-to-all-start.1 = ((bf16[16,64,4096]{2,1,0:T(8,128)(2,1)}), bf16[16,64,4096]{2,1,0:T(8,128)(2,1)}, u32[]{:S(2)}, u32[]{:S(2)}) async-start(bf16[16,64,4096]{2,1,0:T(8,128)(2,1)} %stack.12), calls=%async_computation.2 | async-start | bytes 16777216 | tf_op jit(solution)/shard_map/all_to_all | solution.py:59
  444.8 232.5 %reduce-scatter.5.cloned.1.call-start = ((), (), s32[]{:S(2)}) async-start(), calls=%async_computation.7 | async-start | bytes 8912896 | tf_op jit(solution)/shard_map/reduce_scatter | solution.py:68
  575.4 0.7 copy-start.15
  576.7 4.6 copy-start.1
  581.3 4.1 copy-start.7
  581.3 4.1 copy-start.8
  585.4 91.9 %copy-start.4 = (bf16[64,4096]{1,0:T(8,128)(2,1)S(1)}, bf16[64,4096]{1,0:T(8,128)(2,1)}, u32[]{:S(2)}) copy-start(bf16[64,4096]{1,0:T(8,128)(2,1)} %copy-done.3) | copy-start | bytes 1572868
  585.4 93.0 %copy-start.6 = (bf16[64,4096]{1,0:T(8,128)(2,1)S(1)}, bf16[64,4096]{1,0:T(8,128)(2,1)}, u32[]{:S(2)}) copy-start(bf16[64,4096]{1,0:T(8,128)(2,1)} %copy-done.5) | copy-start | bytes 1572868
Sparse Core Ops, SparseCore 0:
  9.7 121.0 all-gather.2
  132.5 66.6 all-gather.4
  292.0 127.4 reduce-scatter.2
  575.6 101.6 reduce-scatter.4
